TPU v7x, 32 devices: a whole 2x2x4 slice. The times are simulated.
32 devices in a mesh: groups: 2 (over x), frame: 16 (over z, y, core).
Axes of the slice: x: 2, y: 2, z: 4, core: 2. Of those that a mesh axis runs over, the one named last changes fastest.
Arguments:
- latent_images: bfloat16 [64, 4, 240, 256], P(('groups', 'frame')), parts along dimension 0, may hold values from -6 to 6
- initial_group_scale: float32 [256], replicated, may hold values from 0.1 to 1.9
- initial_conv_taps: bfloat16 [3, 3, 256, 256], replicated, may hold values from -0.125 to 0.125
- later_group_scale: float32 [256], replicated, may hold values from 0.1 to 1.9
- later_conv_taps: bfloat16 [3, 3, 256, 256], replicated, may hold values from -0.125 to 0.125
- prenormal_scale_vector: float32 [256], replicated, may hold values from 0.1 to 1.9
- asking_projection_matrix: bfloat16 [256, 256], replicated, may hold values from -0.375 to 0.375
- matching_projection_matrix: bfloat16 [256, 256], replicated, may hold values from -0.375 to 0.375
- content_projection_matrix: bfloat16 [256, 256], replicated, may hold values from -0.375 to 0.375
- closing_projection_matrix: bfloat16 [256, 256], replicated, may hold values from -0.375 to 0.375
- neighbour_time_taps: bfloat16 [3, 256, 256], replicated, may hold values from -0.21875 to 0.21875
- score_sharpness: float32 [4], replicated, may hold values from 0.5 to 120
Outputs:
- result: bfloat16 [64, 4, 240, 256], P(('groups', 'frame')), parts along dimension 0
There are 2 independent parts, one for each index of `groups`. A program takes and returns all parts, laid end to end along the dimension named above; an argument that names none is the same for every part. Nothing has to cross between parts.
All inputs are finite; a program needn't handle non-finite values.
Results may differ from a plain program's by a relative error of at most 0.022.
The roundings to bfloat16 on the way count: a program that leaves them out, or rounds other values in their place, can miss the bound.
Values may be sent and summed in bfloat16 or wider, within the bound.
A program may use at most 64 MiB of HBM per device.

v0:
```python
import math

import jax
import jax.numpy as jnp
from jax import lax
from jax.sharding import PartitionSpec as P

GROUPS = 32


EPSILON = 1e-05


def group_norm(values, gain):
    input_shape = values.shape
    grouped = values.reshape(input_shape[:-1] + (GROUPS, input_shape[-1] // GROUPS))
    average = jnp.mean(grouped, axis=(1, 2, 4), keepdims=True)
    centered = grouped - average
    spread = jnp.mean(centered * centered, axis=(1, 2, 4), keepdims=True)
    return (centered * lax.rsqrt(spread + EPSILON)).reshape(input_shape) * gain


def spatial_conv(active, weight):
    height = active.shape[1]
    breadth = active.shape[2]
    channels = active.shape[3]
    padded = jnp.pad(active, ((0, 0), (1, 1), (1, 1), (0, 0)))
    total = jnp.zeros((active.shape[0] * height * breadth, channels), jnp.float32)
    for row_tap in range(3):
        for col_tap in range(3):
            window = padded[:, row_tap : row_tap + height, col_tap : col_tap + breadth, :].reshape(
                -1, channels
            )
            total = total + jnp.dot(
                window, weight[row_tap, col_tap], preferred_element_type=jnp.float32
            )
    return total.reshape(active.shape)


def spatial_block(
    latent_images, initial_group_scale, initial_conv_taps, later_group_scale, later_conv_taps
):
    first = jax.nn.silu(group_norm(latent_images.astype(jnp.float32), initial_group_scale)).astype(
        jnp.bfloat16
    )
    hidden = spatial_conv(first, initial_conv_taps)
    second = jax.nn.silu(group_norm(hidden, later_group_scale)).astype(jnp.bfloat16)
    return (latent_images.astype(jnp.float32) + spatial_conv(second, later_conv_taps)).astype(
        jnp.bfloat16
    )


def across_time_mixing(
    upscaling_unit_step,
    prenormal_scale_vector,
    asking_projection_matrix,
    matching_projection_matrix,
    content_projection_matrix,
    closing_projection_matrix,
    score_sharpness,
):
    count, pixels, channels = upscaling_unit_step.shape
    number_of_subspaces = score_sharpness.shape[0]
    subspace_dimension = channels // number_of_subspaces
    widened = upscaling_unit_step.astype(jnp.float32)
    average = jnp.mean(widened, axis=-1, keepdims=True)
    centered = widened - average
    spread = jnp.mean(centered * centered, axis=-1, keepdims=True)
    normed = (
        (centered * lax.rsqrt(spread + EPSILON) * prenormal_scale_vector)
        .astype(jnp.bfloat16)
        .reshape(-1, channels)
    )

    def project(weight):
        return (
            jnp.dot(normed, weight, preferred_element_type=jnp.float32)
            .astype(jnp.bfloat16)
            .reshape(count, pixels, number_of_subspaces, subspace_dimension)
        )

    queries = project(asking_projection_matrix)
    keys = project(matching_projection_matrix)
    values = project(content_projection_matrix)
    raw_pair_scores = jnp.einsum(
        "fphd,gphd->phfg", queries, keys, preferred_element_type=jnp.float32
    )
    raw_pair_scores = (
        raw_pair_scores * (score_sharpness / math.sqrt(subspace_dimension))[None, :, None, None]
    )
    probs = jax.nn.softmax(raw_pair_scores, axis=-1).astype(jnp.bfloat16)
    attended = jnp.einsum("phfg,gphd->fphd", probs, values, preferred_element_type=jnp.float32)
    attended = attended.astype(jnp.bfloat16).reshape(-1, channels)
    output = widened + jnp.dot(
        attended, closing_projection_matrix, preferred_element_type=jnp.float32
    ).reshape(upscaling_unit_step.shape)
    return output.astype(jnp.bfloat16)


def time_mix(padded, weight):
    count = padded.shape[0] - 2
    channels = padded.shape[-1]
    center = padded[1 : count + 1]
    total = center.astype(jnp.float32).reshape(-1, channels)
    for offset in range(3):
        total = total + jnp.dot(
            padded[offset : offset + count].reshape(-1, channels),
            weight[offset],
            preferred_element_type=jnp.float32,
        )
    return total.reshape(center.shape).astype(jnp.bfloat16)


def on_device(
    latent_images,
    initial_group_scale,
    initial_conv_taps,
    later_group_scale,
    later_conv_taps,
    prenormal_scale_vector,
    asking_projection_matrix,
    matching_projection_matrix,
    content_projection_matrix,
    closing_projection_matrix,
    neighbour_time_taps,
    score_sharpness,
):
    local = spatial_block(
        latent_images, initial_group_scale, initial_conv_taps, later_group_scale, later_conv_taps
    )
    owners = lax.axis_size("frame")
    channels = local.shape[3]
    split_pixels = local.reshape(
        local.shape[0], owners, local.shape[1] * local.shape[2] // owners, channels
    )
    received = lax.all_to_all(split_pixels, "frame", split_axis=1, concat_axis=0, tiled=True)
    frames_all = received.shape[0]
    pixel_count = received.shape[2]
    upscaling_unit_step = received.reshape(frames_all, pixel_count, channels)
    mixed_result_tensor = across_time_mixing(
        upscaling_unit_step,
        prenormal_scale_vector,
        asking_projection_matrix,
        matching_projection_matrix,
        content_projection_matrix,
        closing_projection_matrix,
        score_sharpness,
    )
    mixed_result_tensor = time_mix(
        jnp.pad(mixed_result_tensor, ((1, 1), (0, 0), (0, 0))), neighbour_time_taps
    )
    owned = mixed_result_tensor.reshape(frames_all, 1, pixel_count, channels)
    returned = lax.all_to_all(owned, "frame", split_axis=0, concat_axis=1, tiled=True)
    return returned.reshape(local.shape)


def solution(mesh):
    in_specs = (
        P(("groups", "frame"), None, None, None),
        P(),
        P(),
        P(),
        P(),
        P(),
        P(),
        P(),
        P(),
        P(),
        P(),
        P(),
    )
    out_specs = P(("groups", "frame"), None, None, None)
    return jax.shard_map(
        on_device, mesh=mesh, in_specs=in_specs, out_specs=out_specs, check_vma=False
    )
```

profile of v0, /device:TPU:0, one launch (start us, length us, event | category | flops | bytes accessed | tf_op | source)
XLA Modules:
  0.0 154.0 jit_solution(5396066368205296608)
XLA Ops:
  0.0 1.5 convert_reduce_fusion
  1.8 1.5 fusion.8
  4.3 2.4 %pad_slice_fusion.8 = (bf16[2,4,240,256]{3,2,1,0:T(8,128)(2,1)S(1)}, bf16[2,4,240,256]{3,2,1,0:T(8,128)(2,1)S(1)}, bf16[2,4,240,256]{3,2,1,0:T(8,128)(2,1)S(1)},...) fusion(bf16[2,4,240,256]{3,2,1,0:T(8,128)(2,1)S(1)} %fusion.15), kind=kLoop, calls=%fused_computation.41 | loop fusion | bytes 8847360 | tf_op jit(solution)/shard_map/slice | solution.py:31
  10.6 1.8 %copy.86 = f32[1920,256]{0,1:T(8,128)} copy(f32[1920,256]{1,0:T(8,128)S(1)} %convolution_add_fusion.11) | data formatting | bytes 3932160 | tf_op jit(solution)/shard_map/add | solution.py:34
  12.4 5.6 %reshape_reshape.6 = f32[2,4,240,32,8]{2,1,0,4,3:T(4,128)} reshape(f32[1920,256]{0,1:T(8,128)} %copy.86) | data formatting | bytes 3932160 | tf_op jit(solution)/shard_map/reshape;reshape | solution.py:16
  18.0 2.1 %reduce_sum.83 = f32[2,32]{0,1:T(8,128)S(1)} reduce(f32[2,4,240,32,8]{2,1,0,4,3:T(4,128)} %reshape_reshape.6, f32[]{:T(128)} %constant.20.clone.1), dimensions={1,2,4}, to_apply=%region_4.5 | reduce | flops 491456 | bytes 1966340 | tf_op jit(solution)/shard_map/reduce_sum | solution.py:17
  20.3 2.4 %multiply_reduce_fusion.1 = f32[2,32]{0,1:T(8,128)S(1)} fusion(f32[2,4,240,32,8]{2,1,0,4,3:T(4,128)} %reshape_reshape.6, f32[2,32]{0,1:T(8,128)S(1)} %copy.88), kind=kLoop, calls=%fused_computation.51 | loop fusion | flops 1474496 | bytes 1966592 | tf_op jit(solution)/shard_map/reduce_sum | solution.py:19
  24.3 2.6 %pad_slice_fusion = (bf16[2,4,240,256]{3,2,1,0:T(8,128)(2,1)S(1)}, bf16[2,4,240,256]{3,2,1,0:T(8,128)(2,1)S(1)}, bf16[2,4,240,256]{3,2,1,0:T(8,128)(2,1)S(1)}, b...) fusion(bf16[2,4,240,256]{3,2,1,0:T(8,128)(2,1)S(1)} %multiply_c, ...), kind=kLoop, calls=%fused_computation.33 | loop fusion | bytes 8847360 | tf_op jit(solution)/shard_map/slice | solution.py:31
  30.9 2.0 %copy.90 = bf16[2,4,240,256]{3,0,2,1:T(2,128)(2,1)} copy(bf16[2,4,240,256]{3,2,1,0:T(8,128)(2,1)S(1)} %fusion.16) | data formatting | bytes 1966080 | tf_op jit(solution)/shard_map/convert_element_type | solution.py:48
  32.9 7.4 %all-to-all-start = ((bf16[2,16,60,256]{3,0,2,1:T(2,128)(2,1)}), bf16[2,16,60,256]{3,0,2,1:T(2,128)(2,1)S(1)}, u32[]{:S(2)}, u32[]{:S(2)}) async-start(bf16[2,16,60,256]{3,0,2,1:T(2,128)(2,1)} %bitcast.39), calls=%async_computation | async-start | bytes 1966080 | tf_op jit(solution)/shard_map/all_to_all | solution.py:136
  40.3 21.8 %all-to-all-done = bf16[2,16,60,256]{3,0,2,1:T(2,128)(2,1)S(1)} async-done(((bf16[2,16,60,256]{3,0,2,1:T(2,128)(2,1)}), bf16[2,16,60,256]{3,0,2,1:T(2,128)(2,1)S(1)}, u32[]{:S(2)}, u32[]{:S(2)}) %all-to-all-start) | async-done | bytes 983072 | tf_op jit(solution)/shard_map/all_to_all | solution.py:136
  62.2 1.1 fusion.27
  63.8 13.5 %multiply_reduce_fusion.2 = f32[16,2,60]{1,2,0:T(8,128)S(1)} fusion(bf16[2,16,60,256]{3,0,2,1:T(2,128)(2,1)S(1)} %all-to-all-done, f32[16,2,60]{1,2,0:T(8,128)S(1)} %copy.95), kind=kLoop, calls=%fused_computation.74 | loop fusion | flops 1964160 | bytes 998400 | tf_op jit(solution)/shard_map/reduce_sum | solution.py:68
  78.7 1.5 reshape.219
  80.3 2.1 %multiply_convert_fusion = bf16[1920,256]{1,0:T(8,128)(2,1)S(1)} fusion(f32[1920,256]{1,0:T(8,128)} %reshape.219, f32[256]{0:T(256)S(1)} %copy-done.11, f32[1920]{0:T(1024)S(1)} %rsqrt.30, f32[1920]{0:T(1024)S(1)} %div.49), kind=kLoop, calls=%fused_computation.73 | loop fusion | flops 1966080 | bytes 2965504 | tf_op jit(solution)/shard_map/convert_element_type | solution.py:71
  82.4 1.4 convolution_convert_fusion.1
  83.8 4.2 %reshape.211 = bf16[32,60,4,64]{3,2,1,0:T(4,128)(2,1)} reshape(bf16[1920,256]{1,0:T(8,128)(2,1)} %convolution_convert_fusion.1) | data formatting | bytes 1966080 | tf_op jit(solution)/shard_map/reshape | solution.py:79
  88.0 1.4 convolution_convert_fusion
  89.4 4.2 %reshape.212 = bf16[32,60,4,64]{3,2,1,0:T(4,128)(2,1)} reshape(bf16[1920,256]{1,0:T(8,128)(2,1)} %convolution_convert_fusion) | data formatting | bytes 1966080 | tf_op jit(solution)/shard_map/reshape | solution.py:79
  93.6 1.4 convolution_convert_fusion.2
  95.0 4.2 %reshape.210 = bf16[32,60,4,64]{3,2,1,0:T(4,128)(2,1)} reshape(bf16[1920,256]{1,0:T(8,128)(2,1)} %convolution_convert_fusion.2) | data formatting | bytes 1966080 | tf_op jit(solution)/shard_map/reshape | solution.py:79
  99.2 3.3 %fusion.20 = f32[60,4,32,32]{2,3,1,0:T(8,128)S(1)} fusion(bf16[32,60,4,64]{3,2,1,0:T(4,128)(2,1)} %reshape.212, bf16[32,60,4,64]{3,2,1,0:T(4,128)(2,1)} %reshape.211), kind=kOutput, calls=%fused_computation.67 | convolution fusion | flops 31457280 | bytes 2949120 | tf_op jit(solution)/shard_map/fphd,gphd->phfg/dot_general | solution.py:85
  102.5 2.0 %fusion.73 = (f32[60,4,32]{2,1,0:T(4,128)S(1)}, f32[60,4,32,32]{2,3,1,0:T(8,128)S(1)}) fusion(f32[60,4,32,32]{2,3,1,0:T(8,128)S(1)} %fusion.20, f32[4]{0:T(128)S(1)} %broadcast_multiply_fusion.3), kind=kOutput, calls=%fused_computation.132 | output fusion | flops 983071 | bytes 1996816 | tf_op jit(solution)/shard_map/sub | solution.py:91
  104.5 1.1 convert_bitcast_fusion.1
  105.6 2.3 %copy.108 = bf16[32,60,4,64]{3,2,1,0:T(4,128)(2,1)} copy(bf16[32,60,4,64]{3,0,2,1:T(8,128)(2,1)S(1)} %convert_bitcast_fusion.1) | data formatting | bytes 1966080 | tf_op jit(solution)/shard_map/dot_general | solution.py:94
  107.9 4.2 %reshape.224 = bf16[32,60,256]{2,1,0:T(8,128)(2,1)} reshape(bf16[32,60,4,64]{3,2,1,0:T(4,128)(2,1)} %copy.108) | data formatting | bytes 1966080 | tf_op jit(solution)/shard_map/dot_general | solution.py:94
  112.1 1.7 %fusion.7 = bf16[32,60,256]{2,1,0:T(8,128)(2,1)S(1)} fusion(f32[16,2,1,60,256]{4,3,1,0,2:T(8,128)S(1)} %copy.91, bf16[32,60,256]{2,1,0:T(8,128)(2,1)} %reshape.224, bf16[256,256]{1,0:T(8,128)(2,1)S(1)} %copy-done.8), kind=kOutput, calls=%fused_computation.50 | convolution fusion | flops 252641280 | bytes 4063232 | tf_op jit(solution)/shard_map/dot_general | solution.py:94
  113.8 1.2 pad_slice_fusion.16
  117.0 1.3 reshape.216
  118.4 1.4 fusion.4
  119.7 1.3 convert_element_type.107
  121.0 30.9 %all_to_all.24 = bf16[32,1,60,256]{3,2,1,0:T(8,128)(2,1)S(1)} all-to-all(bf16[32,1,60,256]{3,2,1,0:T(8,128)(2,1)S(1)} %bitcast.155), channel_id=1, replica_groups=mesh['groups'=2,'frame'=16] {'frame'}, dimensions={0} | all-to-all | bytes 1966080 | tf_op jit(solution)/shard_map/all_to_all | solution.py:153
  (85 shorter events, 16.9 us)
Async XLA Ops:
  0.0 82.4 %copy-start = (bf16[256,256]{1,0:T(8,128)(2,1)S(1)}, bf16[256,256]{1,0:T(8,128)(2,1)}, u32[]{:S(2)}) copy-start(bf16[256,256]{1,0:T(8,128)(2,1)} %param.18) | copy-start | bytes 393220
  0.0 3.7 %copy-start.1 = (bf16[2,4,240,256]{3,2,1,0:T(8,128)(2,1)S(1)}, bf16[2,4,240,256]{3,2,1,0:T(8,128)(2,1)}, u32[]{:S(2)}) copy-start(bf16[2,4,240,256]{3,2,1,0:T(8,128)(2,1)} %param.12) | copy-start | bytes 2949124
  0.0 3.7 %copy-start.10 = (f32[256]{0:T(256)S(1)}, f32[256]{0:T(256)}, u32[]{:S(2)}) copy-start(f32[256]{0:T(256)} %param.13) | copy-start | bytes 3076
  4.3 2.5 %copy-start.3 = (bf16[3,3,256,256]{3,2,1,0:T(8,128)(2,1)S(1)}, bf16[3,3,256,256]{3,2,1,0:T(8,128)(2,1)}, u32[]{:S(2)}) copy-start(bf16[3,3,256,256]{3,2,1,0:T(8,128)(2,1)} %param.14) | copy-start | bytes 3538948
  18.0 5.1 %copy-start.9 = (f32[256]{0:T(256)S(1)}, f32[256]{0:T(256)}, u32[]{:S(2)}) copy-start(f32[256]{0:T(256)} %param.15) | copy-start | bytes 3076
  24.3 2.6 %copy-start.4 = (bf16[3,3,256,256]{3,2,1,0:T(8,128)(2,1)S(1)}, bf16[3,3,256,256]{3,2,1,0:T(8,128)(2,1)}, u32[]{:S(2)}) copy-start(bf16[3,3,256,256]{3,2,1,0:T(8,128)(2,1)} %param.16) | copy-start | bytes 3538948
  30.9 9.4 %copy-start.12 = (f32[4]{0:T(128)S(1)}, f32[4]{0:T(128)}, u32[]{:S(2)}) copy-start(f32[4]{0:T(128)} %param.23) | copy-start | bytes 52
  32.9 29.2 %all-to-all-start = ((bf16[2,16,60,256]{3,0,2,1:T(2,128)(2,1)}), bf16[2,16,60,256]{3,0,2,1:T(2,128)(2,1)S(1)}, u32[]{:S(2)}, u32[]{:S(2)}) async-start(bf16[2,16,60,256]{3,0,2,1:T(2,128)(2,1)} %bitcast.39), calls=%async_computation | async-start | bytes 1966080 | tf_op jit(solution)/shard_map/all_to_all | solution.py:136
  78.7 1.6 %copy-start.11 = (f32[256]{0:T(256)S(1)}, f32[256]{0:T(256)}, u32[]{:S(2)}) copy-start(f32[256]{0:T(256)} %param.17) | copy-start | bytes 3076
  83.8 4.2 %copy-start.6 = (bf16[256,256]{1,0:T(8,128)(2,1)S(1)}, bf16[256,256]{1,0:T(8,128)(2,1)}, u32[]{:S(2)}) copy-start(bf16[256,256]{1,0:T(8,128)(2,1)} %param.19) | copy-start | bytes 393220
  89.4 4.2 %copy-start.7 = (bf16[256,256]{1,0:T(8,128)(2,1)S(1)}, bf16[256,256]{1,0:T(8,128)(2,1)}, u32[]{:S(2)}) copy-start(bf16[256,256]{1,0:T(8,128)(2,1)} %param.20) | copy-start | bytes 393220
  102.5 2.0 %copy-start.2 = (bf16[32,60,4,64]{3,2,1,0:T(4,128)(2,1)S(1)}, bf16[32,60,4,64]{3,2,1,0:T(4,128)(2,1)}, u32[]{:S(2)}) copy-start(bf16[32,60,4,64]{3,2,1,0:T(4,128)(2,1)} %reshape.210) | copy-start | bytes 2949124
  107.9 4.2 %copy-start.8 = (bf16[256,256]{1,0:T(8,128)(2,1)S(1)}, bf16[256,256]{1,0:T(8,128)(2,1)}, u32[]{:S(2)}) copy-start(bf16[256,256]{1,0:T(8,128)(2,1)} %param.21) | copy-start | bytes 393220
  115.2 1.0 copy-start.5
where the time goes:
time: 155 us; the launch traced here: 154 us
  local copies, waits for them, and re-layouts  44.6 us (29%)
  blocking collectives  30.9 us (20%)
  other arithmetic  29.1 us (19%)
  waiting for transfers between devices  21.8 us (14%)
  matrix products  19.8 us (13%)
  starting transfers between devices  7.41 us (5%)
    all_to_all x1, blocking collectives, on_device(): lax.all_to_all(owned, 'frame', split_axis=0, concat_axis=1, tiled=True)  30.9 us
    all_to_all x1, waiting for transfers between devices, on_device(): lax.all_to_all(split_pixels, 'frame', split_axis=1, concat_axis=0, tiled=...  21.8 us
    reduce_sum x1, other arithmetic, across_time_mixing(): spread = jnp.mean(centered * centered, axis=-1, keepdims=True)  13.5 us
    reshape x3, local copies, waits for them, and re-layouts, project(): return jnp.dot(normed, weight, preferred_element_type=jnp.float32).astype...  12.7 us
    dot_general x18, matrix products, spatial_conv(): jnp.dot(window, weight[row_tap, col_tap], preferred_element_type=jnp.floa...  7.45 us
    all_to_all x1, starting transfers between devices, on_device(): lax.all_to_all(split_pixels, 'frame', split_axis=1, concat_axis=0, tiled=...  7.41 us
    dot_general x2, local copies, waits for them, and re-layouts, across_time_mixing(): jnp.dot(attended, closing_projection_matrix, preferred_element_type=jnp.f...  6.48 us
    another operation x1, local copies, waits for them, and re-layouts, group_norm(): values.reshape(input_shape[:-1] + (GROUPS, input_shape[-1] // GROUPS))  5.64 us
  transfers between devices with their start and end apart: 1, of which 1 were waited for; matrix products, arithmetic and copies ran while one was open for 0% of the time, Pallas kernels for 0%

commit v1 on v0

v1 whole, which is shorter than its diff:
```python
import functools
import math

import jax
import jax.numpy as jnp
from jax import lax
from jax.experimental import pallas as pl
from jax.experimental.pallas import tpu as pltpu
from jax.sharding import PartitionSpec as P

GROUPS = 32
EPSILON = 1e-05
SUB = 8
CHUNK = 16
F32 = jnp.float32
BF16 = jnp.bfloat16


def dot(a, b):
    return jnp.dot(a, b, preferred_element_type=F32)


def kernel(
    n,
    per,
    height,
    width,
    own,
    heads,
    x_ref,
    g1_ref,
    w1_ref,
    g2_ref,
    w2_ref,
    pn_ref,
    wq_ref,
    wk_ref,
    wv_ref,
    wo_ref,
    tt_ref,
    sharp_ref,
    out_ref,
    act,
    hid,
    local,
    recv,
    q_s,
    k_s,
    v_s,
    o_s,
    fin,
    back,
    send1,
    recv1,
    send2,
    recv2,
):
    me = lax.axis_index("frame")
    pixels = height * width
    channels = x_ref.shape[-1]
    frames = n * per
    padded = local.shape[2]
    chunks = padded // CHUNK
    rows = frames * SUB
    block = min(rows, 256)

    def peer(j):
        t = (j + 1) // 2
        k = n // 2 + (1 - 2 * (j % 2)) * t
        return lax.rem(me + k, n), lax.rem(me - k + n, n)

    barrier = pltpu.get_barrier_semaphore()

    @pl.loop(0, n - 1)
    def _(j):
        to, _ = peer(j)
        pl.semaphore_signal(
            barrier, inc=1, device_id={"frame": to}, device_id_type=pl.DeviceIdType.MESH
        )

    act[pl.ds(0, width), :] = jnp.zeros((width, 3 * channels), BF16)
    act[pl.ds((height + 1) * width, width), :] = jnp.zeros((width, 3 * channels), BF16)

    ci = lax.broadcasted_iota(jnp.int32, (channels, channels), 0) // (channels // GROUPS)
    cj = lax.broadcasted_iota(jnp.int32, (channels, channels), 1) // (channels // GROUPS)
    same_group = jnp.where(ci == cj, 1.0, 0.0).astype(F32)
    scale = 1.0 / (pixels * (channels // GROUPS))
    col = lax.broadcasted_iota(jnp.int32, (width, channels), 0)

    def group_mean(partial):
        total = jnp.broadcast_to(jnp.sum(partial, axis=0, keepdims=True), (8, channels))
        return (
            jnp.dot(
                total, same_group, preferred_element_type=F32, precision=lax.Precision.HIGHEST
            )[:1]
            * scale
        )

    def row_of(i):
        return pl.ds(pl.multiple_of(i * width, width), width)

    def fold(v):
        return jnp.sum(v.reshape(width // 8, 8, channels), axis=0)

    def norm_silu(load, gain):
        zero = jnp.zeros((8, channels), F32)
        mean = group_mean(
            lax.fori_loop(0, height, lambda i, s: s + fold(load(i)), zero)
        )

        def square(i, s):
            c = load(i) - mean
            return s + fold(c * c)

        inv = lax.rsqrt(group_mean(lax.fori_loop(0, height, square, zero)) + EPSILON)

        @pl.loop(0, height)
        def _(i):
            v = (load(i) - mean) * inv * gain
            y = (v / (1.0 + jnp.exp(-v))).astype(BF16)
            wide = y.astype(F32)
            there = pl.ds(pl.multiple_of((i + 1) * width, width), width)
            act[there, pl.ds(0, channels)] = jnp.where(
                col == 0, 0.0, pltpu.roll(wide, 1, 0)
            ).astype(BF16)
            act[there, pl.ds(channels, channels)] = y
            act[there, pl.ds(2 * channels, channels)] = jnp.where(
                col == width - 1, 0.0, pltpu.roll(wide, width - 1, 0)
            ).astype(BF16)

    def conv(w_ref):
        total = None
        for a in range(3):
            term = dot(
                act[pl.ds(a * width, pixels), :],
                w_ref[pl.ds(a * 3 * channels, 3 * channels), :],
            )
            total = term if total is None else total + term
        return total

    def forward(f, to, source):
        return pltpu.make_async_remote_copy(
            src_ref=local.at[f, to],
            dst_ref=recv.at[source * per + f],
            send_sem=send1.at[f, to],
            recv_sem=recv1.at[f, source],
            device_id={"frame": to},
            device_id_type=pl.DeviceIdType.MESH,
        )

    @pl.loop(0, per)
    def _(f):
        norm_silu(lambda i: x_ref[f, row_of(i), :].astype(F32), g1_ref[...])
        hid[...] = conv(w1_ref)
        norm_silu(lambda i: hid[row_of(i), :], g2_ref[...])
        hid[...] = x_ref[f].astype(F32) + conv(w2_ref)
        for o in range(n):
            v = hid[pl.ds(o * own, own), :]
            if padded > own:
                v = jnp.concatenate([v, jnp.zeros((padded - own, channels), F32)], axis=0)
            local[f, o] = v.astype(BF16)
        recv[me * per + f] = local[f, me]

        @pl.when(f == 0)
        def _():
            pl.semaphore_wait(barrier, n - 1)

        @pl.loop(0, n - 1)
        def _(j):
            to, _ = peer(j)
            forward(f, to, me).start()

    @pl.loop(0, per)
    def _(f):
        @pl.loop(0, n - 1)
        def _(j):
            to, source = peer(j)
            forward(f, to, source).wait_recv()

    lane = lax.broadcasted_iota(jnp.int32, (1, channels), 1) // (channels // heads)
    ri = lax.broadcasted_iota(jnp.int32, (block, rows), 0) % SUB
    rj = lax.broadcasted_iota(jnp.int32, (block, rows), 1) % SUB
    same_pixel = ri == rj
    halves = CHUNK // SUB

    def returning(g, to, source):
        px = pl.ds(pl.multiple_of(g * CHUNK, CHUNK), CHUNK)
        return pltpu.make_async_remote_copy(
            src_ref=fin.at[to, :, px],
            dst_ref=back.at[source, :, px],
            send_sem=send2.at[g, to],
            recv_sem=recv2.at[g, source],
            device_id={"frame": to},
            device_id_type=pl.DeviceIdType.MESH,
        )

    @pl.loop(0, chunks)
    def _(g):
        px = pl.ds(pl.multiple_of(g * CHUNK, CHUNK), CHUNK)
        x = recv[:, px, :].astype(F32).reshape(frames * CHUNK, channels)
        c = x - jnp.mean(x, axis=-1, keepdims=True)
        var = jnp.mean(c * c, axis=-1, keepdims=True)
        normed = (c * lax.rsqrt(var + EPSILON) * pn_ref[...]).astype(BF16)
        for ref, w in ((q_s, wq_ref), (k_s, wk_ref), (v_s, wv_ref)):
            t = dot(normed, w[...]).reshape(frames, CHUNK, channels)
            for half in range(halves):
                ref[half] = (
                    t[:, half * SUB : (half + 1) * SUB].reshape(rows, channels).astype(BF16)
                )

        @pl.loop(0, halves)
        def _(half):
            @pl.loop(0, rows // block)
            def _(b):
                qs = pl.ds(pl.multiple_of(b * block, block), block)
                q = q_s[half, qs, :]
                k = k_s[half]
                v = v_s[half]
                total = None
                for h in range(heads):
                    keep = jnp.where(lane == h, 1.0, 0.0).astype(BF16)
                    s = lax.dot_general(
                        q * keep, k, (((1,), (1,)), ((), ())), preferred_element_type=F32
                    )
                    s = s * (sharp_ref[h] * (1.0 / math.sqrt(channels // heads)))
                    s = jnp.where(same_pixel, s, -jnp.inf)
                    e = jnp.exp(s - jnp.max(s, axis=-1, keepdims=True))
                    p = (e * (1.0 / jnp.sum(e, axis=-1, keepdims=True))).astype(BF16)
                    term = dot(p, v * keep)
                    total = term if total is None else total + term
                o_s[half, qs, :] = total

        attended = jnp.concatenate(
            [o_s[half].reshape(frames, SUB, channels) for half in range(halves)], axis=1
        )
        attended = attended.reshape(frames * CHUNK, channels).astype(BF16)
        x = recv[:, px, :].astype(F32).reshape(frames * CHUNK, channels)
        mixed = (x + dot(attended, wo_ref[...])).astype(BF16)
        edge = jnp.zeros((CHUNK, channels), BF16)
        before = jnp.concatenate([edge, mixed[:-CHUNK]], axis=0)
        after = jnp.concatenate([mixed[CHUNK:], edge], axis=0)
        result = mixed.astype(F32)
        for t, m in enumerate((before, mixed, after)):
            result = result + dot(m, tt_ref[t])
        fin[:, :, px, :] = result.astype(BF16).reshape(n, per, CHUNK, channels)
        back[me, :, px, :] = fin[me, :, px, :]

        @pl.loop(0, n - 1)
        def _(j):
            to, _ = peer(j)
            returning(g, to, me).start()

    @pl.loop(0, chunks)
    def _(g):
        @pl.loop(0, n - 1)
        def _(j):
            to, source = peer(j)
            returning(g, to, source).wait_recv()

    for f in range(per):
        for o in range(n):
            hid[pl.ds(o * own, own), :] = back[o, f].astype(F32)[:own]
        out_ref[f] = hid[...].astype(BF16)

    @pl.loop(0, n - 1)
    def _(j):
        to, source = peer(j)

        @pl.loop(0, per)
        def _(f):
            forward(f, to, source).wait_send()

        @pl.loop(0, chunks)
        def _(g):
            returning(g, to, source).wait_send()


def on_device(n, latent, g1, w1, g2, w2, pn, wq, wk, wv, wo, tt, sharp):
    per, height, width, channels = latent.shape
    pixels = height * width
    own = pixels // n
    padded = -(-own // CHUNK) * CHUNK
    frames = n * per
    heads = sharp.shape[0]
    rows = frames * SUB
    halves = CHUNK // SUB
    chunks = padded // CHUNK
    vmem = pl.BlockSpec(memory_space=pltpu.VMEM)
    out = pl.pallas_call(
        functools.partial(kernel, n, per, height, width, own, heads),
        out_shape=jax.ShapeDtypeStruct((per, pixels, channels), BF16),
        in_specs=[vmem] * 11 + [pl.BlockSpec(memory_space=pltpu.SMEM)],
        out_specs=vmem,
        scratch_shapes=[
            pltpu.VMEM(((height + 2) * width, 3 * channels), BF16),
            pltpu.VMEM((pixels, channels), F32),
            pltpu.VMEM((per, n, padded, channels), BF16),
            pltpu.VMEM((frames, padded, channels), BF16),
            pltpu.VMEM((halves, rows, channels), BF16),
            pltpu.VMEM((halves, rows, channels), BF16),
            pltpu.VMEM((halves, rows, channels), BF16),
            pltpu.VMEM((halves, rows, channels), F32),
            pltpu.VMEM((n, per, padded, channels), BF16),
            pltpu.VMEM((n, per, padded, channels), BF16),
            pltpu.SemaphoreType.DMA((per, n)),
            pltpu.SemaphoreType.DMA((per, n)),
            pltpu.SemaphoreType.DMA((chunks, n)),
            pltpu.SemaphoreType.DMA((chunks, n)),
        ],
        compiler_params=pltpu.CompilerParams(
            collective_id=0, has_side_effects=True, vmem_limit_bytes=60 * 1024 * 1024
        ),
        name="block",
    )(
        latent.reshape(per, pixels, channels),
        g1.reshape(1, channels),
        w1.reshape(9 * channels, channels),
        g2.reshape(1, channels),
        w2.reshape(9 * channels, channels),
        pn.reshape(1, channels),
        wq,
        wk,
        wv,
        wo,
        tt,
        sharp,
    )
    return out.reshape(latent.shape)


def solution(mesh):
    split = P(("groups", "frame"), None, None, None)
    return jax.shard_map(
        functools.partial(on_device, mesh.shape["frame"]),
        mesh=mesh,
        in_specs=(split,) + (P(),) * 11,
        out_specs=split,
        check_vma=False,
    )
```

time: 155 us -> 68.9 us (0.44)
  Pallas kernels: 0 us -> 66.6 us
  local copies, waits for them, and re-layouts: 44.6 us -> 2.21 us
  blocking collectives: 30.9 us -> 0 us
  other arithmetic: 29.1 us -> 0 us
  waiting for transfers between devices: 21.8 us -> 0 us
  matrix products: 19.8 us -> 0 us
  starting transfers between devices: 7.41 us -> 0 us
    pallas_call x0 -> x1, Pallas kernels: none -> 66.6 us  [on_device(): pl.pallas_call(functools.partial(kernel, n, per, height, width, own, head...]
    all_to_all x1 -> x0, blocking collectives: 30.9 us -> none  [on_device(): lax.all_to_all(owned, 'frame', split_axis=0, concat_axis=1, tiled=True)]
    reduce_sum x8 -> x0, other arithmetic: 22.2 us -> none  [the longest x1 13.5 us: across_time_mixing(): spread = jnp.mean(centered * centered, axis=-1, keepdims=True)]
    all_to_all x1 -> x0, waiting for transfers between devices: 21.8 us -> none  [on_device(): lax.all_to_all(split_pixels, 'frame', split_axis=1, concat_axis=0, tiled=...]
    dot_general x27 -> x0, matrix products: 19.8 us -> none  [the longest x18 7.45 us: spatial_conv(): jnp.dot(window, weight[row_tap, col_tap], preferred_element_type=jnp.floa...]
    reshape x7 -> x0, local copies, waits for them, and re-layouts: 15.4 us -> none  [the longest x3 12.7 us: project(): return jnp.dot(normed, weight, preferred_element_type=jnp.float32).astype...]
    all_to_all x1 -> x0, starting transfers between devices: 7.41 us -> none  [on_device(): lax.all_to_all(split_pixels, 'frame', split_axis=1, concat_axis=0, tiled=...]
    dot_general x2 -> x0, local copies, waits for them, and re-layouts: 6.48 us -> none  [across_time_mixing(): jnp.dot(attended, closing_projection_matrix, preferred_element_type=jnp.f...]
  transfers between devices with their start and end apart: 1 -> 0, of which waited for: 1 -> 0; matrix products, arithmetic and copies ran while one was open for 0% -> 0% of each run, Pallas kernels for 0% -> 0%
where the time goes in v1:
time: 68.9 us; the launch traced here: 68.8 us
  Pallas kernels  66.6 us (97%)
  local copies, waits for them, and re-layouts  2.21 us (3%)
    pallas_call x1, Pallas kernels, on_device(): pl.pallas_call(functools.partial(kernel, n, per, height, width, own, head...  66.6 us
    unnamed x1, local copies, waits for them, and re-layouts  2.21 us

profile of v1, /device:TPU:0, one launch (start us, length us, event | category | flops | bytes accessed | tf_op | source)
XLA Modules:
  0.0 68.8 jit_solution(8315924431098915798)
XLA Ops:
  0.0 66.6 %block.1 = bf16[2,960,256]{2,1,0:T(8,128)(2,1)} custom-call(bf16[2,960,256]{2,1,0:T(8,128)(2,1)} %bitcast.10, f32[1,256]{1,0:T(1,128)} %bitcast.11, bf16[2304,256]{1,0:T(8,128)(2,1)} %bitcast.8, f32[1,256]{1,0:T(1,128)} %bitcast.12, bf16[2304,256]{1,0:T(8,128)(2,1)} %bitcast.9, f32[1,256]{1,0:T(1,128)} %bitcast.13, bf16[256,256]{1,0:T(8,128)(2,1)} %wq_ref.1, ...), custom_call_target="tpu_custom_call" | custom-call | tf_op jit(solution)/shard_map/block/pallas_call | solution.py:289
  66.6 2.2 %copy.14 = bf16[2,4,240,256]{3,2,1,0:T(8,128)(2,1)} copy(bf16[2,4,240,256]{3,2,1,0:T(8,128)(2,1)} %bitcast.7) | data formatting | bytes 1966080

commit v2 on v1

--- a/solution.py
+++ b/solution.py
@@ -12,6 +12,7 @@
 EPSILON = 1e-05
 SUB = 8
 CHUNK = 16
+PAIR = 2
 F32 = jnp.float32
 BF16 = jnp.bfloat16
 
@@ -25,21 +26,28 @@
     per,
     height,
     width,
-    own,
     heads,
+    x_hbm,
+    g1_ref,
+    w1_hbm,
+    g2_ref,
+    w2_hbm,
+    pn_ref,
+    wq_hbm,
+    wk_hbm,
+    wv_hbm,
+    wo_hbm,
+    tt_hbm,
+    sharp_ref,
+    out_ref,
     x_ref,
-    g1_ref,
     w1_ref,
-    g2_ref,
     w2_ref,
-    pn_ref,
     wq_ref,
     wk_ref,
     wv_ref,
     wo_ref,
     tt_ref,
-    sharp_ref,
-    out_ref,
     act,
     hid,
     local,
@@ -49,7 +57,8 @@
     v_s,
     o_s,
     fin,
-    back,
+    load,
+    keep_sem,
     send1,
     recv1,
     send2,
@@ -59,8 +68,9 @@
     pixels = height * width
     channels = x_ref.shape[-1]
     frames = n * per
-    padded = local.shape[2]
-    chunks = padded // CHUNK
+    units = pixels // CHUNK
+    chunks = -(-units // n)
+    missing = chunks * n - units
     rows = frames * SUB
     block = min(rows, 256)
 
@@ -68,6 +78,31 @@
         t = (j + 1) // 2
         k = n // 2 + (1 - 2 * (j % 2)) * t
         return lax.rem(me + k, n), lax.rem(me - k + n, n)
+
+    def count(g):
+        return n - missing * (g // (chunks - 1) if chunks > 1 else 1)
+
+    def rows_of(g, o):
+        unit = g * n + (o * count(g)) // n
+        return pl.ds(pl.multiple_of(unit * CHUNK, CHUNK), CHUNK)
+
+    def owns(g, o):
+        return ((o + 1) * count(g)) // n > (o * count(g)) // n
+
+    loads = [pltpu.make_async_copy(x_hbm.at[f], x_ref.at[f], load.at[f]) for f in range(per)]
+    for source, target in (
+        (w1_hbm, w1_ref),
+        (w2_hbm, w2_ref),
+        (wq_hbm, wq_ref),
+        (wk_hbm, wk_ref),
+        (wv_hbm, wv_ref),
+        (wo_hbm, wo_ref),
+        (tt_hbm, tt_ref),
+    ):
+        loads.append(pltpu.make_async_copy(source, target, load.at[len(loads)]))
+    loads = [loads[0], loads[per]] + loads[1:per] + loads[per + 1 :]
+    for copy in loads:
+        copy.start()
 
     barrier = pltpu.get_barrier_semaphore()
 
@@ -128,54 +163,67 @@
                 col == width - 1, 0.0, pltpu.roll(wide, width - 1, 0)
             ).astype(BF16)
 
-    def conv(w_ref):
+    def conv(w_ref, start, size):
         total = None
         for a in range(3):
             term = dot(
-                act[pl.ds(a * width, pixels), :],
+                act[pl.ds(a * width + start, size), :],
                 w_ref[pl.ds(a * 3 * channels, 3 * channels), :],
             )
             total = term if total is None else total + term
         return total
 
-    def forward(f, to, source):
+    def forward(f, g, to, source):
         return pltpu.make_async_remote_copy(
-            src_ref=local.at[f, to],
-            dst_ref=recv.at[source * per + f],
-            send_sem=send1.at[f, to],
-            recv_sem=recv1.at[f, source],
+            src_ref=local.at[f, rows_of(g, to)],
+            dst_ref=recv.at[g, source * per + f],
+            send_sem=send1.at[f, g, to],
+            recv_sem=recv1.at[f, g, source],
             device_id={"frame": to},
             device_id_type=pl.DeviceIdType.MESH,
         )
+
+    loads[0].wait()
 
     @pl.loop(0, per)
     def _(f):
         norm_silu(lambda i: x_ref[f, row_of(i), :].astype(F32), g1_ref[...])
-        hid[...] = conv(w1_ref)
-        norm_silu(lambda i: hid[row_of(i), :], g2_ref[...])
-        hid[...] = x_ref[f].astype(F32) + conv(w2_ref)
-        for o in range(n):
-            v = hid[pl.ds(o * own, own), :]
-            if padded > own:
-                v = jnp.concatenate([v, jnp.zeros((padded - own, channels), F32)], axis=0)
-            local[f, o] = v.astype(BF16)
-        recv[me * per + f] = local[f, me]
 
         @pl.when(f == 0)
         def _():
+            loads[1].wait()
+
+        hid[...] = conv(w1_ref, 0, pixels)
+        norm_silu(lambda i: hid[row_of(i), :], g2_ref[...])
+
+        @pl.when(f == 0)
+        def _():
+            for copy in loads[2:]:
+                copy.wait()
             pl.semaphore_wait(barrier, n - 1)
 
-        @pl.loop(0, n - 1)
-        def _(j):
-            to, _ = peer(j)
-            forward(f, to, me).start()
-
-    @pl.loop(0, per)
-    def _(f):
-        @pl.loop(0, n - 1)
-        def _(j):
-            to, source = peer(j)
-            forward(f, to, source).wait_recv()
+        for first in range(0, chunks, PAIR):
+            last = min(first + PAIR, chunks)
+            start = first * n * CHUNK
+            size = min(last * n * CHUNK, pixels) - start
+            part = pl.ds(start, size)
+            local[f, part, :] = (x_ref[f, part, :].astype(F32) + conv(w2_ref, start, size)).astype(
+                BF16
+            )
+
+            @pl.loop(first, last)
+            def _(g):
+                @pl.loop(0, n - 1)
+                def _(j):
+                    to, _ = peer(j)
+
+                    @pl.when(owns(g, to))
+                    def _():
+                        forward(f, g, to, me).start()
+
+                @pl.when(owns(g, me))
+                def _():
+                    recv[g, me * per + f] = local[f, rows_of(g, me), :]
 
     lane = lax.broadcasted_iota(jnp.int32, (1, channels), 1) // (channels // heads)
     ri = lax.broadcasted_iota(jnp.int32, (block, rows), 0) % SUB
@@ -184,20 +232,29 @@
     halves = CHUNK // SUB
 
     def returning(g, to, source):
-        px = pl.ds(pl.multiple_of(g * CHUNK, CHUNK), CHUNK)
         return pltpu.make_async_remote_copy(
-            src_ref=fin.at[to, :, px],
-            dst_ref=back.at[source, :, px],
+            src_ref=fin.at[g, to],
+            dst_ref=out_ref.at[:, rows_of(g, source)],
             send_sem=send2.at[g, to],
             recv_sem=recv2.at[g, source],
             device_id={"frame": to},
             device_id_type=pl.DeviceIdType.MESH,
         )
 
-    @pl.loop(0, chunks)
-    def _(g):
-        px = pl.ds(pl.multiple_of(g * CHUNK, CHUNK), CHUNK)
-        x = recv[:, px, :].astype(F32).reshape(frames * CHUNK, channels)
+    def keeping(g):
+        return pltpu.make_async_copy(
+            fin.at[g, me], out_ref.at[:, rows_of(g, me)], keep_sem.at[g]
+        )
+
+    def attend(g):
+        @pl.loop(0, per)
+        def _(f):
+            @pl.loop(0, n - 1)
+            def _(j):
+                to, source = peer(j)
+                forward(f, g, to, source).wait_recv()
+
+        x = recv[g].astype(F32).reshape(frames * CHUNK, channels)
         c = x - jnp.mean(x, axis=-1, keepdims=True)
         var = jnp.mean(c * c, axis=-1, keepdims=True)
         normed = (c * lax.rsqrt(var + EPSILON) * pn_ref[...]).astype(BF16)
@@ -234,7 +291,7 @@
             [o_s[half].reshape(frames, SUB, channels) for half in range(halves)], axis=1
         )
         attended = attended.reshape(frames * CHUNK, channels).astype(BF16)
-        x = recv[:, px, :].astype(F32).reshape(frames * CHUNK, channels)
+        x = recv[g].astype(F32).reshape(frames * CHUNK, channels)
         mixed = (x + dot(attended, wo_ref[...])).astype(BF16)
         edge = jnp.zeros((CHUNK, channels), BF16)
         before = jnp.concatenate([edge, mixed[:-CHUNK]], axis=0)
@@ -242,8 +299,8 @@
         result = mixed.astype(F32)
         for t, m in enumerate((before, mixed, after)):
             result = result + dot(m, tt_ref[t])
-        fin[:, :, px, :] = result.astype(BF16).reshape(n, per, CHUNK, channels)
-        back[me, :, px, :] = fin[me, :, px, :]
+        fin[g] = result.astype(BF16).reshape(n, per, CHUNK, channels)
+        keeping(g).start()
 
         @pl.loop(0, n - 1)
         def _(j):
@@ -252,58 +309,74 @@
 
     @pl.loop(0, chunks)
     def _(g):
+        @pl.when(owns(g, me))
+        def _():
+            attend(g)
+
+    @pl.loop(0, chunks)
+    def _(g):
+        @pl.when(owns(g, me))
+        def _():
+            keeping(g).wait()
+
         @pl.loop(0, n - 1)
         def _(j):
             to, source = peer(j)
-            returning(g, to, source).wait_recv()
-
-    for f in range(per):
-        for o in range(n):
-            hid[pl.ds(o * own, own), :] = back[o, f].astype(F32)[:own]
-        out_ref[f] = hid[...].astype(BF16)
-
-    @pl.loop(0, n - 1)
-    def _(j):
-        to, source = peer(j)
-
-        @pl.loop(0, per)
-        def _(f):
-            forward(f, to, source).wait_send()
-
-        @pl.loop(0, chunks)
-        def _(g):
-            returning(g, to, source).wait_send()
+
+            @pl.when(owns(g, source))
+            def _():
+                returning(g, to, source).wait_recv()
+
+            @pl.when(owns(g, me))
+            def _():
+                returning(g, to, source).wait_send()
+
+            @pl.when(owns(g, to))
+            def _():
+                @pl.loop(0, per)
+                def _(f):
+                    forward(f, g, to, source).wait_send()
 
 
 def on_device(n, latent, g1, w1, g2, w2, pn, wq, wk, wv, wo, tt, sharp):
     per, height, width, channels = latent.shape
     pixels = height * width
-    own = pixels // n
-    padded = -(-own // CHUNK) * CHUNK
     frames = n * per
     heads = sharp.shape[0]
     rows = frames * SUB
     halves = CHUNK // SUB
-    chunks = padded // CHUNK
+    chunks = -(-(pixels // CHUNK) // n)
     vmem = pl.BlockSpec(memory_space=pltpu.VMEM)
+    hbm = pl.BlockSpec(memory_space=pl.ANY)
     out = pl.pallas_call(
-        functools.partial(kernel, n, per, height, width, own, heads),
+        functools.partial(kernel, n, per, height, width, heads),
         out_shape=jax.ShapeDtypeStruct((per, pixels, channels), BF16),
-        in_specs=[vmem] * 11 + [pl.BlockSpec(memory_space=pltpu.SMEM)],
-        out_specs=vmem,
+        in_specs=[hbm, vmem, hbm, vmem, hbm, vmem]
+        + [hbm] * 5
+        + [pl.BlockSpec(memory_space=pltpu.SMEM)],
+        out_specs=hbm,
         scratch_shapes=[
+            pltpu.VMEM((per, pixels, channels), BF16),
+            pltpu.VMEM((9 * channels, channels), BF16),
+            pltpu.VMEM((9 * channels, channels), BF16),
+            pltpu.VMEM(wq.shape, BF16),
+            pltpu.VMEM(wk.shape, BF16),
+            pltpu.VMEM(wv.shape, BF16),
+            pltpu.VMEM(wo.shape, BF16),
+            pltpu.VMEM(tt.shape, BF16),
             pltpu.VMEM(((height + 2) * width, 3 * channels), BF16),
             pltpu.VMEM((pixels, channels), F32),
-            pltpu.VMEM((per, n, padded, channels), BF16),
-            pltpu.VMEM((frames, padded, channels), BF16),
+            pltpu.VMEM((per, pixels, channels), BF16),
+            pltpu.VMEM((chunks, frames, CHUNK, channels), BF16),
             pltpu.VMEM((halves, rows, channels), BF16),
             pltpu.VMEM((halves, rows, channels), BF16),
             pltpu.VMEM((halves, rows, channels), BF16),
             pltpu.VMEM((halves, rows, channels), F32),
-            pltpu.VMEM((n, per, padded, channels), BF16),
-            pltpu.VMEM((n, per, padded, channels), BF16),
-            pltpu.SemaphoreType.DMA((per, n)),
-            pltpu.SemaphoreType.DMA((per, n)),
+            pltpu.VMEM((chunks, n, per, CHUNK, channels), BF16),
+            pltpu.SemaphoreType.DMA((per + 7,)),
+            pltpu.SemaphoreType.DMA((chunks,)),
+            pltpu.SemaphoreType.DMA((per, chunks, n)),
+            pltpu.SemaphoreType.DMA((per, chunks, n)),
             pltpu.SemaphoreType.DMA((chunks, n)),
             pltpu.SemaphoreType.DMA((chunks, n)),
         ],

time: 68.9 us -> 63.3 us (0.919)
  Pallas kernels: 66.6 us -> 60.9 us
    pallas_call x1, Pallas kernels: 66.6 us -> 60.9 us  [on_device(): pl.pallas_call(functools.partial(kernel, n, per, height, width, heads), o...]
where the time goes in v2:
time: 63.3 us; the launch traced here: 63.1 us
  Pallas kernels  60.9 us (96%)
  local copies, waits for them, and re-layouts  2.21 us (3%)
    pallas_call x1, Pallas kernels, on_device(): pl.pallas_call(functools.partial(kernel, n, per, height, width, heads), o...  60.9 us
    unnamed x1, local copies, waits for them, and re-layouts  2.21 us

profile of v2, /device:TPU:0, one launch (start us, length us, event | category | flops | bytes accessed | tf_op | source)
XLA Modules:
  0.0 63.1 jit_solution(13965824897825602152)
XLA Ops:
  0.0 60.9 %block.1 = bf16[2,960,256]{2,1,0:T(8,128)(2,1)} custom-call(bf16[2,960,256]{2,1,0:T(8,128)(2,1)} %bitcast.10, f32[1,256]{1,0:T(1,128)} %bitcast.11, bf16[2304,256]{1,0:T(8,128)(2,1)} %bitcast.8, f32[1,256]{1,0:T(1,128)} %bitcast.12, bf16[2304,256]{1,0:T(8,128)(2,1)} %bitcast.9, f32[1,256]{1,0:T(1,128)} %bitcast.13, bf16[256,256]{1,0:T(8,128)(2,1)} %wq_hbm.1, ...), custom_call_target="tpu_custom_call" | custom-call | tf_op jit(solution)/shard_map/block/pallas_call | solution.py:351
  60.9 2.2 %copy.14 = bf16[2,4,240,256]{3,2,1,0:T(8,128)(2,1)} copy(bf16[2,4,240,256]{3,2,1,0:T(8,128)(2,1)} %bitcast.7) | data formatting | bytes 1966080

commit v3 on v2

--- a/solution.py
+++ b/solution.py
@@ -12,7 +12,7 @@
 EPSILON = 1e-05
 SUB = 8
 CHUNK = 16
-PAIR = 2
+PAIR = 1
 F32 = jnp.float32
 BF16 = jnp.bfloat16
 
@@ -116,20 +116,21 @@
     act[pl.ds(0, width), :] = jnp.zeros((width, 3 * channels), BF16)
     act[pl.ds((height + 1) * width, width), :] = jnp.zeros((width, 3 * channels), BF16)
 
-    ci = lax.broadcasted_iota(jnp.int32, (channels, channels), 0) // (channels // GROUPS)
-    cj = lax.broadcasted_iota(jnp.int32, (channels, channels), 1) // (channels // GROUPS)
-    same_group = jnp.where(ci == cj, 1.0, 0.0).astype(F32)
+    place = lax.broadcasted_iota(jnp.int32, (8, channels), 1)
     scale = 1.0 / (pixels * (channels // GROUPS))
     col = lax.broadcasted_iota(jnp.int32, (width, channels), 0)
 
     def group_mean(partial):
         total = jnp.broadcast_to(jnp.sum(partial, axis=0, keepdims=True), (8, channels))
-        return (
-            jnp.dot(
-                total, same_group, preferred_element_type=F32, precision=lax.Precision.HIGHEST
-            )[:1]
-            * scale
-        )
+        step = 1
+        while step < channels // GROUPS:
+            total = total + jnp.where(
+                (place // step) % 2 == 0,
+                pltpu.roll(total, channels - step, 1),
+                pltpu.roll(total, step, 1),
+            )
+            step *= 2
+        return total[:1] * scale
 
     def row_of(i):
         return pl.ds(pl.multiple_of(i * width, width), width)
@@ -152,7 +153,7 @@
         @pl.loop(0, height)
         def _(i):
             v = (load(i) - mean) * inv * gain
-            y = (v / (1.0 + jnp.exp(-v))).astype(BF16)
+            y = (0.5 * v * (1.0 + jnp.tanh(0.5 * v))).astype(BF16)
             wide = y.astype(F32)
             there = pl.ds(pl.multiple_of((i + 1) * width, width), width)
             act[there, pl.ds(0, channels)] = jnp.where(

time: 63.3 us -> 62.4 us (0.986)
  Pallas kernels: 60.9 us -> 60 us
    pallas_call x1, Pallas kernels: 60.9 us -> 60 us  [on_device(): pl.pallas_call(functools.partial(kernel, n, per, height, width, heads), o...]
where the time goes in v3:
time: 62.4 us; the launch traced here: 62.3 us
  Pallas kernels  60 us (96%)
  local copies, waits for them, and re-layouts  2.21 us (4%)
    pallas_call x1, Pallas kernels, on_device(): pl.pallas_call(functools.partial(kernel, n, per, height, width, heads), o...  60 us
    unnamed x1, local copies, waits for them, and re-layouts  2.21 us

profile of v3, /device:TPU:0, one launch (start us, length us, event | category | flops | bytes accessed | tf_op | source)
XLA Modules:
  0.0 62.3 jit_solution(4760344524768260487)
XLA Ops:
  0.0 60.0 %block.1 = bf16[2,960,256]{2,1,0:T(8,128)(2,1)} custom-call(bf16[2,960,256]{2,1,0:T(8,128)(2,1)} %bitcast.10, f32[1,256]{1,0:T(1,128)} %bitcast.11, bf16[2304,256]{1,0:T(8,128)(2,1)} %bitcast.8, f32[1,256]{1,0:T(1,128)} %bitcast.12, bf16[2304,256]{1,0:T(8,128)(2,1)} %bitcast.9, f32[1,256]{1,0:T(1,128)} %bitcast.13, bf16[256,256]{1,0:T(8,128)(2,1)} %wq_hbm.1, ...), custom_call_target="tpu_custom_call" | custom-call | tf_op jit(solution)/shard_map/block/pallas_call | solution.py:352
  60.1 2.2 %copy.14 = bf16[2,4,240,256]{3,2,1,0:T(8,128)(2,1)} copy(bf16[2,4,240,256]{3,2,1,0:T(8,128)(2,1)} %bitcast.7) | data formatting | bytes 1966080
